TPU v7x, 128 devices: a whole 4x4x4 slice. The times are simulated.
128 devices in a mesh: row: 8 (over y, x_lo), col: 16 (over x_hi, z, core).
Axes of the slice: x: 4 (x_hi: 2, x_lo: 2; x = x_hi * 2 + x_lo), y: 4, z: 4, core: 2. Of those that a mesh axis runs over, the one named last changes fastest.
Arguments:
- activations: bfloat16 [2048, 8192], P('col', 'row'), may hold values from -6 to 6
- output_grad: bfloat16 [2048, 8192], P('col', 'row'), may hold values from -1.5 to 1.5
- tile_counts: int32 [32], replicated, may hold values from 16 to 64, as said below
- w_gate: bfloat16 [8192, 15360], P('row', 'col'), may hold values from -0.0625 to 0.0625
- w_up: bfloat16 [8192, 15360], P('row', 'col'), may hold values from -0.0625 to 0.0625
- w_down: bfloat16 [15360, 8192], P('col', 'row'), may hold values from -0.046875 to 0.046875
Outputs:
- input_grad: bfloat16 [2048, 8192], P('col', 'row')
- grad_gate: bfloat16 [8192, 15360], P('row', 'col')
- grad_up: bfloat16 [8192, 15360], P('row', 'col')
- grad_down: bfloat16 [15360, 8192], P('col', 'row')
Inputs may be any that keep to these rules, and one draw needn't show every extreme that they name: `tile_counts`: number of live tokens at the start of each tile of 64 positions; some tile is full and some holds 16.
All inputs are finite; a program needn't handle non-finite values.
Results may differ from a plain program's by a relative error of at most 0.03.
Values may be sent and summed in bfloat16 or wider, within the bound.
No kernel may reach another device: no remote copies, remote signals or barrier semaphores. Data moves between devices by JAX's collectives and lax.ppermute only.
A program may use at most 128 MiB of HBM per device.

v0:
```python
import jax
import jax.numpy as jnp
from jax import lax
from jax.sharding import PartitionSpec as P

TILE = 64


def contract_rows(left, right):
    return lax.dot_general(
        left, right, (((0,), (0,)), ((), ())), preferred_element_type=jnp.float32
    )


def contract_cols(left, right):
    return lax.dot_general(
        left, right, (((1,), (1,)), ((), ())), preferred_element_type=jnp.float32
    )


def swiglu_back(totals, columns):
    gate_sum = totals[:, :columns]
    up_sum = totals[:, columns : 2 * columns]
    back_sum = totals[:, 2 * columns :]
    sigmoid_gate = jax.nn.sigmoid(gate_sum)
    hidden = (gate_sum * sigmoid_gate * up_sum).astype(jnp.bfloat16)
    d_gate = (back_sum * up_sum * sigmoid_gate * (1.0 + gate_sum * (1.0 - sigmoid_gate))).astype(
        jnp.bfloat16
    )
    d_up = (back_sum * gate_sum * sigmoid_gate).astype(jnp.bfloat16)
    return (hidden, d_gate, d_up)


def shards(activations, output_grad, tile_counts, w_gate, w_up, w_down):
    own_rows = activations.shape[0]
    columns = w_gate.shape[1]
    tile_total = tile_counts.shape[0]
    position = lax.axis_index("col") * own_rows + lax.iota(jnp.int32, own_rows)
    in_tile = (position // TILE)[:, None] == lax.iota(jnp.int32, tile_total)[None, :]
    row_limit = jnp.sum(jnp.where(in_tile, tile_counts[None, :], 0), axis=1)
    kept_rows = position % TILE < row_limit
    live_grad = jnp.where(kept_rows[:, None], output_grad, jnp.zeros_like(output_grad))
    inputs_all, grads_all = (
        lax.all_gather(activations, "col", axis=0, tiled=True),
        lax.all_gather(live_grad, "col", axis=0, tiled=True),
    )
    gate_part = jnp.dot(inputs_all, w_gate, preferred_element_type=jnp.float32)
    up_part = jnp.dot(inputs_all, w_up, preferred_element_type=jnp.float32)
    back_part = contract_cols(grads_all, w_down)
    totals = lax.psum_scatter(
        jnp.concatenate([gate_part, up_part, back_part], axis=1).astype(jnp.bfloat16),
        "row",
        scatter_dimension=0,
        tiled=True,
    ).astype(jnp.float32)
    hidden_share, gate_share, up_share = swiglu_back(totals, columns)
    hidden, d_gate, d_up = (
        lax.all_gather(hidden_share, "row", axis=0, tiled=True),
        lax.all_gather(gate_share, "row", axis=0, tiled=True),
        lax.all_gather(up_share, "row", axis=0, tiled=True),
    )
    grad_gate = contract_rows(inputs_all, d_gate).astype(jnp.bfloat16)
    grad_up = contract_rows(inputs_all, d_up).astype(jnp.bfloat16)
    grad_down = contract_rows(hidden, grads_all).astype(jnp.bfloat16)
    input_grad = lax.psum_scatter(
        (contract_cols(d_gate, w_gate) + contract_cols(d_up, w_up)).astype(jnp.bfloat16),
        "col",
        scatter_dimension=0,
        tiled=True,
    )
    return (input_grad, grad_gate, grad_up, grad_down)


def solution(mesh):
    in_specs = (
        P("col", "row"),
        P("col", "row"),
        P(),
        P("row", "col"),
        P("row", "col"),
        P("col", "row"),
    )
    out_specs = (P("col", "row"), P("row", "col"), P("row", "col"), P("col", "row"))
    return jax.shard_map(shards, mesh=mesh, in_specs=in_specs, out_specs=out_specs, check_vma=False)
```

profile of v0, /device:TPU:0, one launch (start us, length us, event | category | flops | bytes accessed | tf_op | source)
XLA Modules:
  0.0 740.1 jit_solution(12108002158446484)
XLA Ops:
  7.2 0.0 copy-start
  7.2 0.0 all-gather.6.cloned.1.call-start
  7.2 0.7 all-gather.6.cloned.1.call-update
  7.9 0.0 all-gather.8.cloned.1.call-start
  8.0 0.7 select_reduce_fusion
  8.7 1.7 broadcast_select_fusion
  10.5 0.0 all-gather.8.cloned.1.call-update
  10.5 0.0 reduce-scatter.3.cloned.1.call-start
  10.6 57.9 %all-gather.6.cloned.1.call-done = bf16[2048,1024]{1,0:T(8,128)(2,1)} async-done(((bf16[128,1024]{1,0:T(8,128)(2,1)}), bf16[2048,1024]{1,0:T(8,128)(2,1)}) %all-gather.6.cloned.1.call-update) | async-done | bytes 4194320 | tf_op jit(solution)/shard_map/all_gather | solution.py:44
  68.4 0.0 copy-start.4
  68.4 9.1 %convolution_convert_fusion.1 = bf16[2048,960]{0,1:T(8,128)(2,1)} fusion(bf16[2048,1024]{1,0:T(8,128)(2,1)} %all-gather.6.cloned.1.call-done, bf16[1024,960]{0,1:T(8,128)(2,1)} %param.10), kind=kOutput, calls=%fused_computation.3 | convolution fusion | flops 4028497920 | bytes 10092544 | tf_op jit(solution)/shard_map/dot_general | solution.py:48
  77.5 0.0 copy-done
  77.5 0.0 copy-done.4
  77.5 5.9 convolution_convert_fusion.2
  83.4 41.2 %all-gather.8.cloned.1.call-done = bf16[2048,1024]{1,0:T(8,128)(2,1)} async-done(((bf16[128,1024]{1,0:T(8,128)(2,1)}), bf16[2048,1024]{1,0:T(8,128)(2,1)}) %all-gather.8.cloned.1.call-update) | async-done | bytes 4194320 | tf_op jit(solution)/shard_map/all_gather | solution.py:45
  124.7 0.0 copy-start.2
  124.7 0.0 copy-start.3
  124.7 7.2 convolution_convert_fusion
  131.9 0.0 copy-done.2
  131.9 0.0 copy-done.3
  131.9 19.8 %pad_maximum_fusion = bf16[2048,2880]{0,1:T(8,128)(2,1)} fusion(bf16[2048,960]{0,1:T(8,128)(2,1)S(1)} %convolution_convert_fusion, bf16[2048,960]{0,1:T(8,128)(2,1)S(1)} %copy-done.2, bf16[2048,960]{0,1:T(8,128)(2,1)S(1)} %copy-done.3), kind=kLoop, calls=%fused_computation | loop fusion | flops 35389440 | bytes 23592960 | tf_op jit(solution)/shard_map/concatenate | solution.py:51
  151.8 0.0 reduce-scatter.3.cloned.1.call-update
  151.8 0.2 all-gather.10.cloned.1.call-start
  152.0 230.9 %reduce-scatter.3.cloned.1.call-done = bf16[256,2880]{0,1:T(8,128)(2,1)} async-done(((bf16[2048,2880]{0,1:T(8,128)(2,1)}), bf16[256,2880]{0,1:T(8,128)(2,1)}) %reduce-scatter.3.cloned.1.call-update) | async-done | bytes 1474576 | tf_op jit(solution)/shard_map/reduce_scatter | solution.py:50
  382.9 1.6 convert_element_type.31
  384.5 1.7 multiply_convert_fusion
  386.3 0.0 all-gather.10.cloned.1.call-update
  386.3 0.0 all-gather.12.cloned.1.call-start
  386.3 0.5 all-gather.12.cloned.1.call-update
  386.9 0.0 all-gather.14.cloned.1.call-start
  386.9 0.5 all-gather.14.cloned.1.call-update
  387.5 0.0 reduce-scatter.5.cloned.1.call-start
  387.5 84.4 %all-gather.10.cloned.1.call-done = bf16[2048,960]{0,1:T(8,128)(2,1)} async-done(((bf16[256,960]{0,1:T(8,128)(2,1)}), bf16[2048,960]{0,1:T(8,128)(2,1)}) %all-gather.10.cloned.1.call-update) | async-done | bytes 3932176 | tf_op jit(solution)/shard_map/all_gather | solution.py:59
  471.9 8.9 %fusion.1 = f32[2048,1024]{1,0:T(8,128)} fusion(bf16[2048,960]{0,1:T(8,128)(2,1)} %all-gather.10.cloned.1.call-done, bf16[1024,960]{0,1:T(8,128)(2,1)S(1)} %copy-done), kind=kOutput, calls=%fused_computation.22 | convolution fusion | flops 4026531840 | bytes 14286848 | tf_op jit(solution)/shard_map/dot_general | solution.py:16
  480.8 78.6 %all-gather.12.cloned.1.call-done = bf16[2048,960]{0,1:T(8,128)(2,1)} async-done(((bf16[256,960]{0,1:T(8,128)(2,1)}), bf16[2048,960]{0,1:T(8,128)(2,1)}) %all-gather.12.cloned.1.call-update) | async-done | bytes 3932176 | tf_op jit(solution)/shard_map/all_gather | solution.py:60
  559.4 11.6 %add_convert_fusion = bf16[2048,1024]{1,0:T(8,128)(2,1)} fusion(f32[2048,1024]{1,0:T(8,128)} %fusion.1, bf16[2048,960]{0,1:T(8,128)(2,1)} %all-gather.12.cloned.1.call-done, bf16[1024,960]{0,1:T(8,128)(2,1)} %param.10), kind=kOutput, calls=%fused_computation.1 | convolution fusion | flops 4030726144 | bytes 18481152 | tf_op jit(solution)/shard_map/dot_general | solution.py:16
  571.1 0.0 reduce-scatter.5.cloned.1.call-update
  571.1 0.0 copy-start.5
  571.1 0.0 copy-start.6
  571.1 9.1 %convert_bitcast_fusion = bf16[1024,960]{0,1:T(8,128)(2,1)} fusion(bf16[2048,960]{0,1:T(8,128)(2,1)} %all-gather.12.cloned.1.call-done, bf16[2048,1024]{1,0:T(8,128)(2,1)} %all-gather.6.cloned.1.call-done), kind=kOutput, calls=%fused_computation.5 | convolution fusion | flops 4027514880 | bytes 10092544 | tf_op jit(solution)/shard_map/dot_general | solution.py:10
  580.2 0.0 copy-done.5
  580.2 0.0 copy-done.6
  580.2 5.4 convert_bitcast_fusion.1
  585.6 61.3 %all-gather.14.cloned.1.call-done = bf16[2048,960]{0,1:T(8,128)(2,1)} async-done(((bf16[256,960]{0,1:T(8,128)(2,1)}), bf16[2048,960]{0,1:T(8,128)(2,1)}) %all-gather.14.cloned.1.call-update) | async-done | bytes 3932176 | tf_op jit(solution)/shard_map/all_gather | solution.py:58
  646.9 0.0 copy-start.1
  646.9 9.0 %convolution_convert_fusion.3 = bf16[960,1024]{1,0:T(8,128)(2,1)} fusion(bf16[2048,960]{0,1:T(8,128)(2,1)} %all-gather.14.cloned.1.call-done, bf16[2048,1024]{1,0:T(8,128)(2,1)} %all-gather.8.cloned.1.call-done), kind=kOutput, calls=%fused_computation.7 | convolution fusion | flops 4027514880 | bytes 10092544 | tf_op jit(solution)/shard_map/dot_general | solution.py:10
  655.9 77.3 %reduce-scatter.5.cloned.1.call-done = bf16[128,1024]{1,0:T(8,128)(2,1)} async-done(((bf16[2048,1024]{1,0:T(8,128)(2,1)}), bf16[128,1024]{1,0:T(8,128)(2,1)}) %reduce-scatter.5.cloned.1.call-update) | async-done | bytes 262160 | tf_op jit(solution)/shard_map/reduce_scatter | solution.py:65
  733.2 0.0 copy-done.1
  (2 shorter events, 0.0 us)
Async XLA Ops:
  7.2 70.3 %copy-start = (bf16[1024,960]{0,1:T(8,128)(2,1)S(1)}, bf16[1024,960]{0,1:T(8,128)(2,1)}, u32[]{:S(2)}) copy-start(bf16[1024,960]{0,1:T(8,128)(2,1)} %param.9) | copy-start | bytes 5898244
  7.2 61.2 %all-gather.6.cloned.1.call-start = ((), (), s32[]{:S(2)}) async-start(), calls=%async_computation.2 | async-start | bytes 4456448 | tf_op jit(solution)/shard_map/all_gather | solution.py:44
  7.9 116.7 %all-gather.8.cloned.1.call-start = ((), (), s32[]{:S(2)}) async-start(), calls=%async_computation.3 | async-start | bytes 4456448 | tf_op jit(solution)/shard_map/all_gather | solution.py:45
  10.5 372.4 %reduce-scatter.3.cloned.1.call-start = ((), (), s32[]{:S(2)}) async-start(), calls=%async_computation.4 | async-start | bytes 13271040 | tf_op jit(solution)/shard_map/reduce_scatter | solution.py:50
  68.4 9.1 %copy-start.4 = (bf16[2048,1024]{1,0:T(8,128)(2,1)S(1)}, bf16[2048,1024]{1,0:T(8,128)(2,1)}, u32[]{:S(2)}) copy-start(bf16[2048,1024]{1,0:T(8,128)(2,1)} %all-gather.6.cloned.1.call-done) | copy-start | bytes 12582916
  124.7 7.2 copy-start.2
  124.7 7.2 copy-start.3
  151.8 320.1 %all-gather.10.cloned.1.call-start = ((), (), s32[]{:S(2)}) async-start(), calls=%async_computation.5 | async-start | bytes 4423680 | tf_op jit(solution)/shard_map/all_gather | solution.py:59
  386.3 173.1 %all-gather.12.cloned.1.call-start = ((), (), s32[]{:S(2)}) async-start(), calls=%async_computation.6 | async-start | bytes 4423680 | tf_op jit(solution)/shard_map/all_gather | solution.py:60
  386.9 260.0 %all-gather.14.cloned.1.call-start = ((), (), s32[]{:S(2)}) async-start(), calls=%async_computation.8 | async-start | bytes 4423680 | tf_op jit(solution)/shard_map/all_gather | solution.py:58
  387.5 345.8 %reduce-scatter.5.cloned.1.call-start = ((), (), s32[]{:S(2)}) async-start(), calls=%async_computation.7 | async-start | bytes 4456448 | tf_op jit(solution)/shard_map/reduce_scatter | solution.py:65
  571.1 9.1 %copy-start.5 = (bf16[2048,1024]{1,0:T(8,128)(2,1)S(1)}, bf16[2048,1024]{1,0:T(8,128)(2,1)}, u32[]{:S(2)}) copy-start(bf16[2048,1024]{1,0:T(8,128)(2,1)} %all-gather.6.cloned.1.call-done) | copy-start | bytes 12582916
  571.1 9.1 %copy-start.6 = (bf16[2048,960]{0,1:T(8,128)(2,1)S(1)}, bf16[2048,960]{0,1:T(8,128)(2,1)}, u32[]{:S(2)}) copy-start(bf16[2048,960]{0,1:T(8,128)(2,1)} %all-gather.10.cloned.1.call-done) | copy-start | bytes 11796484
  646.9 86.3 %copy-start.1 = (bf16[1024,960]{0,1:T(8,128)(2,1)S(1)}, bf16[1024,960]{0,1:T(8,128)(2,1)}, u32[]{:S(2)}) copy-start(bf16[1024,960]{0,1:T(8,128)(2,1)} %param.9) | copy-start | bytes 5898244
Sparse Core Ops, SparseCore 0:
  10.5 57.8 all-gather.5
  71.5 53.1 all-gather.7
  151.9 230.9 reduce-scatter.2
  386.4 85.4 all-gather.9
  473.9 85.4 all-gather.11
  561.4 85.4 all-gather.13
  651.5 81.6 reduce-scatter.4
where the time goes:
time: 740 us
  waiting for transfers between devices  633 us (86%)
  matrix products  66.3 us (9%)
  other arithmetic  25.7 us (3%)
  between operations  14.2 us (2%)
    reduce_scatter x1, waiting for transfers between devices, shards(): lax.psum_scatter(jnp.concatenate([gate_part, up_part, back_part], axis=1)...  231 us
    all_gather x1, waiting for transfers between devices, shards(): lax.all_gather(gate_share, 'row', axis=0, tiled=True)  84.4 us
    all_gather x1, waiting for transfers between devices, shards(): lax.all_gather(up_share, 'row', axis=0, tiled=True)  78.6 us
    reduce_scatter x1, waiting for transfers between devices, shards(): lax.psum_scatter((contract_cols(d_gate, w_gate) + contract_cols(d_up, w_u...  77.3 us
    all_gather x1, waiting for transfers between devices, shards(): lax.all_gather(hidden_share, 'row', axis=0, tiled=True)  61.3 us
    all_gather x1, waiting for transfers between devices, shards(): lax.all_gather(activations, 'col', axis=0, tiled=True)  57.9 us
    all_gather x1, waiting for transfers between devices, shards(): lax.all_gather(live_grad, 'col', axis=0, tiled=True)  41.2 us
    dot_general x3, matrix products, contract_cols(): lax.dot_general(left, right, (((1,), (1,)), ((), ())), preferred_element_...  27.8 us
  transfers between devices with their start and end apart: 7, of which 7 were waited for; matrix products, arithmetic and copies ran while one was open for 8% of the time, Pallas kernels for 0%

commit v1 on v0

v1 whole, which is shorter than its diff:
```python
import jax
import jax.numpy as jnp
from jax import lax
from jax.sharding import Mesh, PartitionSpec as P

TILE = 64
GROUPS = 4
BF = jnp.bfloat16
F32 = jnp.float32


def dot(left, right, dims):
    return lax.dot_general(left, right, ((dims[:1], dims[1:]), ((), ())), preferred_element_type=F32)


def shift(value, axis, size, step):
    return lax.ppermute(value, axis, [(i, (i + step) % size) for i in range(size)])


def gather_col(value, z_first):
    if z_first:
        blocks = [value] + [shift(value, "z", 4, -k) for k in (1, 2, 3)]
        near = jnp.concatenate(blocks, axis=0)
        far = shift(near, "xh", 2, 1)
    else:
        pair = jnp.concatenate([value, shift(value, "xh", 2, 1)], axis=0)
        moved = [pair] + [shift(pair, "z", 4, -k) for k in (1, 2, 3)]
        rows = value.shape[0]
        near = jnp.concatenate([m[:rows] for m in moved], axis=0)
        far = jnp.concatenate([m[rows:] for m in moved], axis=0)
    half = jnp.concatenate([near, far], axis=0)
    return jnp.concatenate([half, shift(half, "c", 2, 1)], axis=0)


def scatter_col(part):
    rows = part.shape[0] // 16
    half = part.shape[0] // 2
    own = part[:half].astype(BF).astype(F32) + shift(part[half:].astype(BF), "c", 2, 1).astype(F32)
    quarter = half // 2
    own = own[:quarter] + shift(own[quarter:].astype(BF), "xh", 2, 1).astype(F32)
    out = own[:rows]
    for k in (1, 2, 3):
        out = out + shift(own[k * rows : (k + 1) * rows].astype(BF), "z", 4, k).astype(F32)
    return out.astype(BF)


def scatter_row_y(parts, low, rows):
    def block(k, width, skip=0):
        start = low + k * 2 * rows + skip
        return jnp.stack([p[start : start + width] for p in parts])

    total = block(0, 2 * rows).astype(F32)
    for k in (1, 2, 3):
        total = total + shift(block(k, 2 * rows), "y", 4, k).astype(F32)
    return total[:, :rows] + shift(total[:, rows:].astype(BF), "xl", 2, 1).astype(F32)


def scatter_row_x(parts, low, rows):
    far = jnp.stack([p[low + 4 * rows : low + 8 * rows] for p in parts])
    near = jnp.stack([p[low : low + 4 * rows] for p in parts])
    total = near.astype(F32) + shift(far, "xl", 2, 1).astype(F32)
    out = total[:, :rows]
    for k in (1, 2, 3):
        out = out + shift(total[:, k * rows : (k + 1) * rows].astype(BF), "y", 4, k).astype(F32)
    return out


def gather_row_y(share):
    pair = jnp.concatenate([share, shift(share, "xl", 2, 1)], axis=1)
    return [pair] + [shift(pair, "y", 4, -k) for k in (1, 2, 3)]


def gather_row_x(share):
    near = jnp.concatenate([share] + [shift(share, "y", 4, -k) for k in (1, 2, 3)], axis=1)
    return [near, shift(near, "xl", 2, 1)]


def swiglu_back(totals):
    gate_sum, up_sum, back_sum = totals[0], totals[1], totals[2]
    sigmoid_gate = jax.nn.sigmoid(gate_sum)
    hidden = gate_sum * sigmoid_gate * up_sum
    d_gate = back_sum * up_sum * sigmoid_gate * (1.0 + gate_sum * (1.0 - sigmoid_gate))
    d_up = back_sum * gate_sum * sigmoid_gate
    return jnp.stack([hidden.astype(BF), d_gate.astype(BF), d_up.astype(BF)])


def to_relative(value, y, xl, rows_y, rows_x):
    first = value[: 8 * rows_y].reshape(4, 2, rows_y, -1)
    second = value[8 * rows_y :].reshape(2, 4, rows_x, -1)
    first = jnp.where(xl == 0, first, first[:, ::-1])
    second = jnp.where(xl == 0, second, second[::-1])
    first = lax.dynamic_slice_in_dim(jnp.concatenate([first, first[:3]], 0), y, 4, 0)
    second = lax.dynamic_slice_in_dim(jnp.concatenate([second, second[:, :3]], 1), y, 4, 1)
    width = value.shape[1]
    return jnp.concatenate([first.reshape(-1, width), second.reshape(-1, width)], 0)


def from_relative(value, y, xl, rows_y, rows_x):
    first = value[: 8 * rows_y].reshape(4, 2, rows_y, -1)
    second = value[8 * rows_y :].reshape(2, 4, rows_x, -1)
    first = jnp.where(xl == 0, first, first[:, ::-1])
    second = jnp.where(xl == 0, second, second[::-1])
    back = (4 - y) % 4
    first = lax.dynamic_slice_in_dim(jnp.concatenate([first, first[:3]], 0), back, 4, 0)
    second = lax.dynamic_slice_in_dim(jnp.concatenate([second, second[:, :3]], 1), back, 4, 1)
    width = value.shape[1]
    return jnp.concatenate([first.reshape(-1, width), second.reshape(-1, width)], 0)


def shards(activations, output_grad, tile_counts, w_gate, w_up, w_down):
    own_rows, width = activations.shape
    tiles = own_rows // TILE
    slots = TILE // GROUPS
    y, xl = lax.axis_index("y"), lax.axis_index("xl")
    col = lax.axis_index(("xh", "z", "c"))
    position = lax.iota(jnp.int32, own_rows)
    in_tile = (col * tiles + position // TILE)[:, None] == lax.iota(jnp.int32, tile_counts.shape[0])[None, :]
    row_limit = jnp.sum(jnp.where(in_tile, tile_counts[None, :], 0), axis=1)
    kept_rows = position % TILE < row_limit
    live_grad = jnp.where(kept_rows[:, None], output_grad, jnp.zeros_like(output_grad))
    acts = activations.reshape(tiles, GROUPS, slots, width)
    grads = live_grad.reshape(tiles, GROUPS, slots, width)
    chunk = 16 * tiles * slots
    rows_y = 3 * chunk // 64
    rows_x = chunk // 8 - rows_y
    wg = wu = wd = None
    out_grads = []
    for j in range(GROUPS):
        x = gather_col(acts[:, j].reshape(tiles * slots, width), True)
        g = gather_col(grads[:, j].reshape(tiles * slots, width), False)
        x = to_relative(x, y, xl, rows_y, rows_x)
        g = to_relative(g, y, xl, rows_y, rows_x)
        parts = (
            dot(x, w_gate, (1, 0)).astype(BF),
            dot(x, w_up, (1, 0)).astype(BF),
            dot(g, w_down, (1, 1)).astype(BF),
        )
        share_y = swiglu_back(scatter_row_y(parts, 0, rows_y))
        share_x = swiglu_back(scatter_row_x(parts, 8 * rows_y, rows_x))
        blocks = gather_row_y(share_y) + gather_row_x(share_x)
        hidden, d_gate, d_up = (jnp.concatenate([b[i] for b in blocks], axis=0) for i in range(3))
        part = (dot(d_gate, w_gate, (1, 1)) + dot(d_up, w_up, (1, 1))).astype(BF)
        out_grads.append(scatter_col(from_relative(part, y, xl, rows_y, rows_x)))
        new_g, new_u, new_d = dot(x, d_gate, (0, 0)), dot(x, d_up, (0, 0)), dot(hidden, g, (0, 0))
        wg, wu, wd = (new_g, new_u, new_d) if wg is None else (wg + new_g, wu + new_u, wd + new_d)
    input_grad = jnp.stack([o.reshape(tiles, slots, width) for o in out_grads], axis=1).reshape(own_rows, width)
    return (input_grad, wg.astype(BF), wu.astype(BF), wd.astype(BF))


def solution(mesh):
    fine = Mesh(mesh.devices.reshape(4, 2, 2, 4, 2), ("y", "xl", "xh", "z", "c"))
    row, col = ("y", "xl"), ("xh", "z", "c")
    in_specs = (P(col, row), P(col, row), P(), P(row, col), P(row, col), P(col, row))
    out_specs = (P(col, row), P(row, col), P(row, col), P(col, row))
    return jax.shard_map(shards, mesh=fine, in_specs=in_specs, out_specs=out_specs, check_vma=False)
```

time: 740 us -> 538 us (0.73); the launches traced: 740 us -> 528 us
  waiting for transfers between devices: 633 us -> 253 us
  starting transfers between devices: 0.46 us -> 167 us
  local copies, waits for them, and re-layouts: 0.03 us -> 26.8 us
  matrix products: 66.3 us -> 54.1 us
  between operations: 14.2 us -> 3.86 us
    all_gather x5 -> x0, waiting for transfers between devices: 323 us -> none  [the longest x1 84.4 us: shards(): lax.all_gather(gate_share, 'row', axis=0, tiled=True)]
    reduce_scatter x2 -> x0, waiting for transfers between devices: 308 us -> none  [the longest x1 231 us: shards(): lax.psum_scatter(jnp.concatenate([gate_part, up_part, back_part], axis=1)...]
    ppermute x0 -> x124, waiting for transfers between devices: none -> 253 us  [shift(): lax.ppermute(value, axis, [(i, (i + step) % size) for i in range(size)])]
    ppermute x0 -> x124, starting transfers between devices: none -> 167 us  [shift(): lax.ppermute(value, axis, [(i, (i + step) % size) for i in range(size)])]
    unnamed x14 -> x172, local copies, waits for them, and re-layouts: 0.03 us -> 18.6 us
    concatenate x1 -> x46, other arithmetic: 19.8 us -> 6.43 us  [the longest x8 2.03 us: to_relative(): jnp.concatenate([second, second[:, :3]], 1)]
    dot_general x8 -> x32, matrix products: 66.3 us -> 54.1 us  [dot(): lax.dot_general(left, right, ((dims[:1], dims[1:]), ((), ())), preferred_...]
  transfers between devices with their start and end apart: 7 -> 124, of which waited for: 7 -> 54; matrix products, arithmetic and copies ran while one was open for 8% -> 15% of each run, Pallas kernels for 0% -> 0%
where the time goes in v1:
time: 538 us; the launch traced here: 528 us
  waiting for transfers between devices  253 us (47%)
  starting transfers between devices  167 us (31%)
  matrix products  54.1 us (10%)
  local copies, waits for them, and re-layouts  26.8 us (5%)
  other arithmetic  22.7 us (4%)
    ppermute x124, waiting for transfers between devices, shift(): lax.ppermute(value, axis, [(i, (i + step) % size) for i in range(size)])  253 us
    ppermute x124, starting transfers between devices, shift(): lax.ppermute(value, axis, [(i, (i + step) % size) for i in range(size)])  167 us
    dot_general x32, matrix products, dot(): lax.dot_general(left, right, ((dims[:1], dims[1:]), ((), ())), preferred_...  54.1 us
    unnamed x172, local copies, waits for them, and re-layouts  18.6 us
  transfers between devices with their start and end apart: 124, of which 54 were waited for; matrix products, arithmetic and copies ran while one was open for 15% of the time, Pallas kernels for 0%

profile of v1, /device:TPU:0, one launch (start us, length us, event | category | flops | bytes accessed | tf_op | source)
XLA Modules:
  0.0 527.6 jit_solution(5655806261026556386)
XLA Ops:
  1.8 4.2 collective-permute-start
  9.0 3.1 collective-permute-start.5
  22.2 3.1 collective-permute-start.67
  27.7 3.2 collective-permute-start.62
  39.6 3.2 collective-permute-start.6
  61.4 3.0 collective-permute-start.3
  72.7 3.1 collective-permute-done.34
  110.1 3.0 collective-permute-start.11
  117.0 3.2 collective-permute-done.10
  121.3 5.8 %collective-permute-done.11 = bf16[3,48,960]{2,1,0:T(8,128)(2,1)S(1)} collective-permute-done((bf16[3,48,960]{2,1,0:T(8,128)(2,1)S(1)}, bf16[3,48,960]{2,1,0:T(8,128)(2,1)S(1)}, u32[]{:S(2)}, u32[]{:S(2)}) %collective-permute-start.11) | collective-permute-done | bytes 276512 | tf_op jit(solution)/shard_map/ppermute | solution.py:17
  127.2 2.9 collective-permute-start.73
  132.8 3.4 collective-permute-start.74
  136.4 3.4 collective-permute-done.42
  139.8 3.0 collective-permute-start.104
  146.9 5.6 %collective-permute-done.73 = bf16[3,48,960]{2,1,0:T(8,128)(2,1)S(1)} collective-permute-done((bf16[3,48,960]{2,1,0:T(8,128)(2,1)S(1)}, bf16[3,48,960]{2,1,0:T(8,128)(2,1)S(1)}, u32[]{:S(2)}, u32[]{:S(2)}) %collective-permute-start.73) | collective-permute-done | bytes 276512 | tf_op jit(solution)/shard_map/ppermute | solution.py:17
  157.8 6.4 %collective-permute-done.104 = bf16[3,48,960]{2,1,0:T(8,128)(2,1)S(1)} collective-permute-done((bf16[3,48,960]{2,1,0:T(8,128)(2,1)S(1)}, bf16[3,48,960]{2,1,0:T(8,128)(2,1)S(1)}, u32[]{:S(2)}, u32[]{:S(2)}) %collective-permute-start.104) | collective-permute-done | bytes 276512 | tf_op jit(solution)/shard_map/ppermute | solution.py:17
  166.5 56.0 %collective-permute-done.13 = bf16[3,24,960]{2,1,0:T(8,128)(2,1)S(1)} collective-permute-done((bf16[3,24,960]{2,1,0:T(8,128)(2,1)S(1)}, bf16[3,24,960]{2,1,0:T(8,128)(2,1)S(1)}, u32[]{:S(2)}, u32[]{:S(2)}) %collective-permute-start.13) | collective-permute-done | bytes 138272 | tf_op jit(solution)/shard_map/ppermute | solution.py:17
  240.7 3.5 collective-permute-done.107
  248.0 4.5 collective-permute-done.16
  252.5 3.1 collective-permute-start.46
  255.7 3.6 collective-permute-done.17
  261.4 7.8 %collective-permute-done.47 = bf16[3,48,960]{2,1,0:T(8,128)(2,1)S(1)} collective-permute-done((bf16[3,48,960]{2,1,0:T(8,128)(2,1)S(1)}, bf16[3,48,960]{2,1,0:T(8,128)(2,1)S(1)}, u32[]{:S(2)}, u32[]{:S(2)}) %collective-permute-start.47) | collective-permute-done | bytes 276512 | tf_op jit(solution)/shard_map/ppermute | solution.py:17
  271.1 5.0 collective-permute-done.48
  278.6 8.7 %collective-permute-done.78 = bf16[3,48,960]{2,1,0:T(8,128)(2,1)S(1)} collective-permute-done((bf16[3,48,960]{2,1,0:T(8,128)(2,1)S(1)}, bf16[3,48,960]{2,1,0:T(8,128)(2,1)S(1)}, u32[]{:S(2)}, u32[]{:S(2)}) %collective-permute-start.78) | collective-permute-done | bytes 276512 | tf_op jit(solution)/shard_map/ppermute | solution.py:17
  287.6 4.0 collective-permute-done.79
  291.6 3.3 collective-permute-start.109
  295.1 7.7 %collective-permute-done.109 = bf16[3,48,960]{2,1,0:T(8,128)(2,1)S(1)} collective-permute-done((bf16[3,48,960]{2,1,0:T(8,128)(2,1)S(1)}, bf16[3,48,960]{2,1,0:T(8,128)(2,1)S(1)}, u32[]{:S(2)}, u32[]{:S(2)}) %collective-permute-start.109) | collective-permute-done | bytes 276512 | tf_op jit(solution)/shard_map/ppermute | solution.py:17
  304.0 6.2 %collective-permute-done.110 = bf16[3,48,960]{2,1,0:T(8,128)(2,1)S(1)} collective-permute-done((bf16[3,48,960]{2,1,0:T(8,128)(2,1)S(1)}, bf16[3,48,960]{2,1,0:T(8,128)(2,1)S(1)}, u32[]{:S(2)}, u32[]{:S(2)}) %collective-permute-start.110) | collective-permute-done | bytes 276512 | tf_op jit(solution)/shard_map/ppermute | solution.py:17
  316.8 3.7 collective-permute-start.51
  321.1 4.9 collective-permute-done.19
  328.5 7.1 %collective-permute-done.50 = bf16[3,40,960]{2,1,0:T(8,128)(2,1)S(1)} collective-permute-done((bf16[3,40,960]{2,1,0:T(8,128)(2,1)S(1)}, bf16[3,40,960]{2,1,0:T(8,128)(2,1)S(1)}, u32[]{:S(2)}, u32[]{:S(2)}) %collective-permute-start.50) | collective-permute-done | bytes 230432 | tf_op jit(solution)/shard_map/ppermute | solution.py:17
  339.1 7.0 %collective-permute-done.81 = bf16[3,40,960]{2,1,0:T(8,128)(2,1)S(1)} collective-permute-done((bf16[3,40,960]{2,1,0:T(8,128)(2,1)S(1)}, bf16[3,40,960]{2,1,0:T(8,128)(2,1)S(1)}, u32[]{:S(2)}, u32[]{:S(2)}) %collective-permute-start.81) | collective-permute-done | bytes 230432 | tf_op jit(solution)/shard_map/ppermute | solution.py:17
  350.6 10.9 %collective-permute-done.112 = bf16[3,40,960]{2,1,0:T(8,128)(2,1)S(1)} collective-permute-done((bf16[3,40,960]{2,1,0:T(8,128)(2,1)S(1)}, bf16[3,40,960]{2,1,0:T(8,128)(2,1)S(1)}, u32[]{:S(2)}, u32[]{:S(2)}) %collective-permute-start.112) | collective-permute-done | bytes 230432 | tf_op jit(solution)/shard_map/ppermute | solution.py:17
  361.5 3.2 collective-permute-start.53
  366.0 6.0 %collective-permute-start.84 = (bf16[3,40,960]{2,1,0:T(8,128)(2,1)S(1)}, bf16[3,40,960]{2,1,0:T(8,128)(2,1)S(1)}, u32[]{:S(2)}, u32[]{:S(2)}) collective-permute-start(bf16[3,40,960]{2,1,0:T(8,128)(2,1)S(1)} %pad_maximum_fusion.61), channel_id=1, source_target_pairs={{0,96},{32,0},{64,32},{96,64},{1,97},{33,1},{65,33},{97,65},{2,98}... | collective-permute-start | bytes 691208 | tf_op jit(solution)/shard_map/ppermute | solution.py:17
  372.1 3.5 collective-permute-done.24
  376.2 3.6 collective-permute-start.115
  393.0 15.1 %collective-permute-done.25 = bf16[3,160,960]{2,1,0:T(8,128)(2,1)S(1)} collective-permute-done((bf16[3,160,960]{2,1,0:T(8,128)(2,1)S(1)}, bf16[3,160,960]{2,1,0:T(8,128)(2,1)S(1)}, u32[]{:S(2)}, u32[]{:S(2)}) %collective-permute-start.25) | collective-permute-done | bytes 921632 | tf_op jit(solution)/shard_map/ppermute | solution.py:17
  409.4 17.8 %collective-permute-done.56 = bf16[3,160,960]{2,1,0:T(8,128)(2,1)S(1)} collective-permute-done((bf16[3,160,960]{2,1,0:T(8,128)(2,1)S(1)}, bf16[3,160,960]{2,1,0:T(8,128)(2,1)S(1)}, u32[]{:S(2)}, u32[]{:S(2)}) %collective-permute-start.56) | collective-permute-done | bytes 921632 | tf_op jit(solution)/shard_map/ppermute | solution.py:17
  434.7 3.1 collective-permute-done.87
  446.4 3.1 fusion.87
  449.9 3.1 fusion.85
  467.9 4.1 add_convert_fusion.1
  472.0 6.7 %add_convert_fusion.2 = bf16[1024,960]{0,1:T(8,128)(2,1)} fusion(f32[1024,960]{0,1:T(8,128)} %fusion.85, f32[1024,960]{0,1:T(8,128)S(1)} %fusion.89, f32[1024,960]{0,1:T(8,128)} %fusion.87, bf16[512,960]{1,0:T(8,128)(2,1)} %copy-done.19, bf16[320,1024]{1,0:T(8,128)(2,1)S(1)} %bitcast.538, bf16[192,1024]{1,0:T(8,128)(2,1)S(1)} %bitcast.550), kind=kOutput, calls=%fused_computation.2 | convolution fusion | flops 1012662272 | bytes 15794176 | tf_op jit(solution)/shard_map/dot_general | solution.py:13
  478.7 2.8 add_convert_fusion
  483.8 2.8 collective-permute-start.27
  490.0 2.8 collective-permute-start.89
  502.2 3.6 collective-permute-done.89
  (645 shorter events, 235.5 us)
Async XLA Ops:
  1.8 17.4 %collective-permute-start = (bf16[32,1024]{1,0:T(8,128)(2,1)S(1)}, bf16[32,1024]{1,0:T(8,128)(2,1)S(1)}, u32[]{:S(2)}, u32[]{:S(2)}) collective-permute-start(bf16[32,1024]{1,0:T(8,128)(2,1)S(1)} %bitcast.631), channel_id=1, source_target_pairs={{0,6},{2,0},{4,2},{6,4},{1,7},{3,1},{5,3},{7,5},{8,14},{10,8},{12,... | collective-permute-start | bytes 196616 | tf_op jit(solution)/shard_map/ppermute | solution.py:17
  5.9 16.3 %collective-permute-start.1 = (bf16[32,1024]{1,0:T(8,128)(2,1)S(1)}, bf16[32,1024]{1,0:T(8,128)(2,1)}, u32[]{:S(2)}, u32[]{:S(2)}) collective-permute-start(bf16[32,1024]{1,0:T(8,128)(2,1)S(1)} %bitcast.632), channel_id=1, source_target_pairs={{0,4},{2,6},{4,0},{6,2},{1,5},{3,7},{5,1},{7,3},{8,12},{10,14},{12... | collective-permute-start | bytes 196616 | tf_op jit(solution)/shard_map/ppermute | solution.py:17
  6.0 16.3 %collective-permute-start.2 = (bf16[32,1024]{1,0:T(8,128)(2,1)S(1)}, bf16[32,1024]{1,0:T(8,128)(2,1)S(1)}, u32[]{:S(2)}, u32[]{:S(2)}) collective-permute-start(bf16[32,1024]{1,0:T(8,128)(2,1)S(1)} %bitcast.633), channel_id=1, source_target_pairs={{0,2},{2,4},{4,6},{6,0},{1,3},{3,5},{5,7},{7,1},{8,10},{10,12},{12... | collective-permute-start | bytes 196616 | tf_op jit(solution)/shard_map/ppermute | solution.py:17
  12.1 15.6 %collective-permute-start.36 = (bf16[32,1024]{1,0:T(8,128)(2,1)S(1)}, bf16[32,1024]{1,0:T(8,128)(2,1)S(1)}, u32[]{:S(2)}, u32[]{:S(2)}) collective-permute-start(bf16[32,1024]{1,0:T(8,128)(2,1)S(1)} %bitcast.610), channel_id=1, source_target_pairs={{0,8},{8,0},{1,9},{9,1},{2,10},{10,2},{3,11},{11,3},{4,12},{12,4},... | collective-permute-start | bytes 196616 | tf_op jit(solution)/shard_map/ppermute | solution.py:17
  72.2 14.9 %collective-permute-start.40 = (bf16[256,1024]{1,0:T(8,128)(2,1)S(1)}, bf16[256,1024]{1,0:T(8,128)(2,1)S(1)}, u32[]{:S(2)}, u32[]{:S(2)}) collective-permute-start(bf16[256,1024]{1,0:T(8,128)(2,1)S(1)} %constant_dynamic-update-slice_fusion.38), channel_id=1, source_target_pairs={{0,1},{1,0},{2,3},{3,2},{4,5},{5,4},{6,7},{7,6},{8,9},{9,8},{10,11... | collective-permute-start | bytes 1572872 | tf_op jit(solution)/shard_map/ppermute | solution.py:17
  89.1 15.8 %collective-permute-start.97 = (bf16[256,1024]{1,0:T(8,128)(2,1)S(1)}, bf16[256,1024]{1,0:T(8,128)(2,1)S(1)}, u32[]{:S(2)}, u32[]{:S(2)}) collective-permute-start(bf16[256,1024]{1,0:T(8,128)(2,1)S(1)} %constant_dynamic-update-slice_fusion.81), channel_id=1, source_target_pairs={{0,1},{1,0},{2,3},{3,2},{4,5},{5,4},{6,7},{7,6},{8,9},{9,8},{10,11... | collective-permute-start | bytes 1572872 | tf_op jit(solution)/shard_map/ppermute | solution.py:17
  110.1 17.1 %collective-permute-start.11 = (bf16[3,48,960]{2,1,0:T(8,128)(2,1)S(1)}, bf16[3,48,960]{2,1,0:T(8,128)(2,1)S(1)}, u32[]{:S(2)}, u32[]{:S(2)}) collective-permute-start(bf16[3,48,960]{2,1,0:T(8,128)(2,1)S(1)} %pad_maximum_fusion.39), channel_id=1, source_target_pairs={{0,64},{32,96},{64,0},{96,32},{1,65},{33,97},{65,1},{97,33},{2,66}... | collective-permute-start | bytes 829448 | tf_op jit(solution)/shard_map/ppermute | solution.py:17
  114.5 18.2 %collective-permute-start.41 = (bf16[3,48,960]{2,1,0:T(8,128)(2,1)S(1)}, bf16[3,48,960]{2,1,0:T(8,128)(2,1)S(1)}, u32[]{:S(2)}, u32[]{:S(2)}) collective-permute-start(bf16[3,48,960]{2,1,0:T(8,128)(2,1)S(1)} %pad_maximum_fusion.42), channel_id=1, source_target_pairs={{0,32},{32,64},{64,96},{96,0},{1,33},{33,65},{65,97},{97,1},{2,34}... | collective-permute-start | bytes 829448 | tf_op jit(solution)/shard_map/ppermute | solution.py:17
  115.3 24.5 %collective-permute-start.42 = (bf16[3,48,960]{2,1,0:T(8,128)(2,1)S(1)}, bf16[3,48,960]{2,1,0:T(8,128)(2,1)S(1)}, u32[]{:S(2)}, u32[]{:S(2)}) collective-permute-start(bf16[3,48,960]{2,1,0:T(8,128)(2,1)S(1)} %pad_maximum_fusion.43), channel_id=1, source_target_pairs={{0,64},{32,96},{64,0},{96,32},{1,65},{33,97},{65,1},{97,33},{2,66}... | collective-permute-start | bytes 829448 | tf_op jit(solution)/shard_map/ppermute | solution.py:17
  120.2 19.7 %collective-permute-start.43 = (bf16[3,48,960]{2,1,0:T(8,128)(2,1)S(1)}, bf16[3,48,960]{2,1,0:T(8,128)(2,1)S(1)}, u32[]{:S(2)}, u32[]{:S(2)}) collective-permute-start(bf16[3,48,960]{2,1,0:T(8,128)(2,1)S(1)} %pad_maximum_fusion.44), channel_id=1, source_target_pairs={{0,96},{32,0},{64,32},{96,64},{1,97},{33,1},{65,33},{97,65},{2,98}... | collective-permute-start | bytes 829448 | tf_op jit(solution)/shard_map/ppermute | solution.py:17
  127.1 18.2 %collective-permute-start.72 = (bf16[3,48,960]{2,1,0:T(8,128)(2,1)S(1)}, bf16[3,48,960]{2,1,0:T(8,128)(2,1)S(1)}, u32[]{:S(2)}, u32[]{:S(2)}) collective-permute-start(bf16[3,48,960]{2,1,0:T(8,128)(2,1)S(1)} %pad_maximum_fusion.46), channel_id=1, source_target_pairs={{0,32},{32,64},{64,96},{96,0},{1,33},{33,65},{65,97},{97,1},{2,34}... | collective-permute-start | bytes 829448 | tf_op jit(solution)/shard_map/ppermute | solution.py:17
  127.2 25.3 %collective-permute-start.73 = (bf16[3,48,960]{2,1,0:T(8,128)(2,1)S(1)}, bf16[3,48,960]{2,1,0:T(8,128)(2,1)S(1)}, u32[]{:S(2)}, u32[]{:S(2)}) collective-permute-start(bf16[3,48,960]{2,1,0:T(8,128)(2,1)S(1)} %pad_maximum_fusion.47), channel_id=1, source_target_pairs={{0,64},{32,96},{64,0},{96,32},{1,65},{33,97},{65,1},{97,33},{2,66}... | collective-permute-start | bytes 829448 | tf_op jit(solution)/shard_map/ppermute | solution.py:17
  132.8 21.0 %collective-permute-start.74 = (bf16[3,48,960]{2,1,0:T(8,128)(2,1)S(1)}, bf16[3,48,960]{2,1,0:T(8,128)(2,1)S(1)}, u32[]{:S(2)}, u32[]{:S(2)}) collective-permute-start(bf16[3,48,960]{2,1,0:T(8,128)(2,1)S(1)} %pad_maximum_fusion.48), channel_id=1, source_target_pairs={{0,96},{32,0},{64,32},{96,64},{1,97},{33,1},{65,33},{97,65},{2,98}... | collective-permute-start | bytes 829448 | tf_op jit(solution)/shard_map/ppermute | solution.py:17
  139.8 16.8 %collective-permute-start.103 = (bf16[3,48,960]{2,1,0:T(8,128)(2,1)S(1)}, bf16[3,48,960]{2,1,0:T(8,128)(2,1)S(1)}, u32[]{:S(2)}, u32[]{:S(2)}) collective-permute-start(bf16[3,48,960]{2,1,0:T(8,128)(2,1)S(1)} %pad_maximum_fusion.50), channel_id=1, source_target_pairs={{0,32},{32,64},{64,96},{96,0},{1,33},{33,65},{65,97},{97,1},{2,34}... | collective-permute-start | bytes 829448 | tf_op jit(solution)/shard_map/ppermute | solution.py:17
  139.8 24.4 %collective-permute-start.104 = (bf16[3,48,960]{2,1,0:T(8,128)(2,1)S(1)}, bf16[3,48,960]{2,1,0:T(8,128)(2,1)S(1)}, u32[]{:S(2)}, u32[]{:S(2)}) collective-permute-start(bf16[3,48,960]{2,1,0:T(8,128)(2,1)S(1)} %pad_maximum_fusion.51), channel_id=1, source_target_pairs={{0,64},{32,96},{64,0},{96,32},{1,65},{33,97},{65,1},{97,33},{2,66}... | collective-permute-start | bytes 829448 | tf_op jit(solution)/shard_map/ppermute | solution.py:17
  145.3 20.1 %collective-permute-start.105 = (bf16[3,48,960]{2,1,0:T(8,128)(2,1)S(1)}, bf16[3,48,960]{2,1,0:T(8,128)(2,1)S(1)}, u32[]{:S(2)}, u32[]{:S(2)}) collective-permute-start(bf16[3,48,960]{2,1,0:T(8,128)(2,1)S(1)} %pad_maximum_fusion.52), channel_id=1, source_target_pairs={{0,96},{32,0},{64,32},{96,64},{1,97},{33,1},{65,33},{97,65},{2,98}... | collective-permute-start | bytes 829448 | tf_op jit(solution)/shard_map/ppermute | solution.py:17
  152.5 157.8 %collective-permute-start.18 = (bf16[3,160,960]{2,1,0:T(8,128)(2,1)S(1)}, bf16[3,160,960]{2,1,0:T(8,128)(2,1)S(1)}, u32[]{:S(2)}, u32[]{:S(2)}) collective-permute-start(bf16[3,160,960]{2,1,0:T(8,128)(2,1)S(1)} %pad_maximum_fusion.8), channel_id=1, source_target_pairs={{0,16},{16,0},{1,17},{17,1},{2,18},{18,2},{3,19},{19,3},{4,20},{20... | collective-permute-start | bytes 2764808 | tf_op jit(solution)/shard_map/ppermute | solution.py:17
  153.8 158.1 %collective-permute-start.49 = (bf16[3,160,960]{2,1,0:T(8,128)(2,1)S(1)}, bf16[3,160,960]{2,1,0:T(8,128)(2,1)S(1)}, u32[]{:S(2)}, u32[]{:S(2)}) collective-permute-start(bf16[3,160,960]{2,1,0:T(8,128)(2,1)S(1)} %pad_maximum_fusion.10), channel_id=1, source_target_pairs={{0,16},{16,0},{1,17},{17,1},{2,18},{18,2},{3,19},{19,3},{4,20},{20... | collective-permute-start | bytes 2764808 | tf_op jit(solution)/shard_map/ppermute | solution.py:17
  156.6 158.6 %collective-permute-start.80 = (bf16[3,160,960]{2,1,0:T(8,128)(2,1)S(1)}, bf16[3,160,960]{2,1,0:T(8,128)(2,1)S(1)}, u32[]{:S(2)}, u32[]{:S(2)}) collective-permute-start(bf16[3,160,960]{2,1,0:T(8,128)(2,1)S(1)} %pad_maximum_fusion.12), channel_id=1, source_target_pairs={{0,16},{16,0},{1,17},{17,1},{2,18},{18,2},{3,19},{19,3},{4,20},{20... | collective-permute-start | bytes 2764808 | tf_op jit(solution)/shard_map/ppermute | solution.py:17
  164.2 58.3 %collective-permute-start.13 = (bf16[3,24,960]{2,1,0:T(8,128)(2,1)S(1)}, bf16[3,24,960]{2,1,0:T(8,128)(2,1)S(1)}, u32[]{:S(2)}, u32[]{:S(2)}) collective-permute-start(bf16[3,24,960]{2,1,0:T(8,128)(2,1)S(1)} %slice.1979), channel_id=1, source_target_pairs={{0,16},{16,0},{1,17},{17,1},{2,18},{18,2},{3,19},{19,3},{4,20},{20... | collective-permute-start | bytes 414728 | tf_op jit(solution)/shard_map/ppermute | solution.py:17
  165.5 60.2 %collective-permute-start.44 = (bf16[3,24,960]{2,1,0:T(8,128)(2,1)S(1)}, bf16[3,24,960]{2,1,0:T(8,128)(2,1)S(1)}, u32[]{:S(2)}, u32[]{:S(2)}) collective-permute-start(bf16[3,24,960]{2,1,0:T(8,128)(2,1)S(1)} %slice.1978), channel_id=1, source_target_pairs={{0,16},{16,0},{1,17},{17,1},{2,18},{18,2},{3,19},{19,3},{4,20},{20... | collective-permute-start | bytes 414728 | tf_op jit(solution)/shard_map/ppermute | solution.py:17
  260.4 15.7 %collective-permute-start.48 = (bf16[3,48,960]{2,1,0:T(8,128)(2,1)S(1)}, bf16[3,48,960]{2,1,0:T(8,128)(2,1)S(1)}, u32[]{:S(2)}, u32[]{:S(2)}) collective-permute-start(bf16[3,48,960]{2,1,0:T(8,128)(2,1)S(1)} %pad_maximum_fusion.45), channel_id=1, source_target_pairs={{0,32},{32,64},{64,96},{96,0},{1,33},{33,65},{65,97},{97,1},{2,34}... | collective-permute-start | bytes 829448 | tf_op jit(solution)/shard_map/ppermute | solution.py:17
  294.9 15.3 %collective-permute-start.110 = (bf16[3,48,960]{2,1,0:T(8,128)(2,1)S(1)}, bf16[3,48,960]{2,1,0:T(8,128)(2,1)S(1)}, u32[]{:S(2)}, u32[]{:S(2)}) collective-permute-start(bf16[3,48,960]{2,1,0:T(8,128)(2,1)S(1)} %pad_maximum_fusion.53), channel_id=1, source_target_pairs={{0,32},{32,64},{64,96},{96,0},{1,33},{33,65},{65,97},{97,1},{2,34}... | collective-permute-start | bytes 829448 | tf_op jit(solution)/shard_map/ppermute | solution.py:17
  310.8 15.2 %collective-permute-start.19 = (bf16[3,40,960]{2,1,0:T(8,128)(2,1)S(1)}, bf16[3,40,960]{2,1,0:T(8,128)(2,1)S(1)}, u32[]{:S(2)}, u32[]{:S(2)}) collective-permute-start(bf16[3,40,960]{2,1,0:T(8,128)(2,1)S(1)} %get-tuple-element.116), channel_id=1, source_target_pairs={{0,32},{32,64},{64,96},{96,0},{1,33},{33,65},{65,97},{97,1},{2,34}... | collective-permute-start | bytes 691208 | tf_op jit(solution)/shard_map/ppermute | solution.py:17
  311.9 16.2 %collective-permute-start.21 = (bf16[3,40,960]{2,1,0:T(8,128)(2,1)S(1)}, bf16[3,40,960]{2,1,0:T(8,128)(2,1)S(1)}, u32[]{:S(2)}, u32[]{:S(2)}) collective-permute-start(bf16[3,40,960]{2,1,0:T(8,128)(2,1)S(1)} %get-tuple-element.117), channel_id=1, source_target_pairs={{0,96},{32,0},{64,32},{96,64},{1,97},{33,1},{65,33},{97,65},{2,98}... | collective-permute-start | bytes 691208 | tf_op jit(solution)/shard_map/ppermute | solution.py:17
  315.2 20.4 %collective-permute-start.50 = (bf16[3,40,960]{2,1,0:T(8,128)(2,1)S(1)}, bf16[3,40,960]{2,1,0:T(8,128)(2,1)S(1)}, u32[]{:S(2)}, u32[]{:S(2)}) collective-permute-start(bf16[3,40,960]{2,1,0:T(8,128)(2,1)S(1)} %get-tuple-element.119), channel_id=1, source_target_pairs={{0,32},{32,64},{64,96},{96,0},{1,33},{33,65},{65,97},{97,1},{2,34}... | collective-permute-start | bytes 691208 | tf_op jit(solution)/shard_map/ppermute | solution.py:17
  316.8 18.8 %collective-permute-start.51 = (bf16[3,40,960]{2,1,0:T(8,128)(2,1)S(1)}, bf16[3,40,960]{2,1,0:T(8,128)(2,1)S(1)}, u32[]{:S(2)}, u32[]{:S(2)}) collective-permute-start(bf16[3,40,960]{2,1,0:T(8,128)(2,1)S(1)} %get-tuple-element.121), channel_id=1, source_target_pairs={{0,64},{32,96},{64,0},{96,32},{1,65},{33,97},{65,1},{97,33},{2,66}... | collective-permute-start | bytes 691208 | tf_op jit(solution)/shard_map/ppermute | solution.py:17
  326.0 20.1 %collective-permute-start.81 = (bf16[3,40,960]{2,1,0:T(8,128)(2,1)S(1)}, bf16[3,40,960]{2,1,0:T(8,128)(2,1)S(1)}, u32[]{:S(2)}, u32[]{:S(2)}) collective-permute-start(bf16[3,40,960]{2,1,0:T(8,128)(2,1)S(1)} %get-tuple-element.122), channel_id=1, source_target_pairs={{0,32},{32,64},{64,96},{96,0},{1,33},{33,65},{65,97},{97,1},{2,34}... | collective-permute-start | bytes 691208 | tf_op jit(solution)/shard_map/ppermute | solution.py:17
  328.1 18.1 %collective-permute-start.82 = (bf16[3,40,960]{2,1,0:T(8,128)(2,1)S(1)}, bf16[3,40,960]{2,1,0:T(8,128)(2,1)S(1)}, u32[]{:S(2)}, u32[]{:S(2)}) collective-permute-start(bf16[3,40,960]{2,1,0:T(8,128)(2,1)S(1)} %get-tuple-element.124), channel_id=1, source_target_pairs={{0,64},{32,96},{64,0},{96,32},{1,65},{33,97},{65,1},{97,33},{2,66}... | collective-permute-start | bytes 691208 | tf_op jit(solution)/shard_map/ppermute | solution.py:17
  335.6 25.9 %collective-permute-start.112 = (bf16[3,40,960]{2,1,0:T(8,128)(2,1)S(1)}, bf16[3,40,960]{2,1,0:T(8,128)(2,1)S(1)}, u32[]{:S(2)}, u32[]{:S(2)}) collective-permute-start(bf16[3,40,960]{2,1,0:T(8,128)(2,1)S(1)} %get-tuple-element.125), channel_id=1, source_target_pairs={{0,32},{32,64},{64,96},{96,0},{1,33},{33,65},{65,97},{97,1},{2,34}... | collective-permute-start | bytes 691208 | tf_op jit(solution)/shard_map/ppermute | solution.py:17
  337.6 23.9 %collective-permute-start.113 = (bf16[3,40,960]{2,1,0:T(8,128)(2,1)S(1)}, bf16[3,40,960]{2,1,0:T(8,128)(2,1)S(1)}, u32[]{:S(2)}, u32[]{:S(2)}) collective-permute-start(bf16[3,40,960]{2,1,0:T(8,128)(2,1)S(1)} %get-tuple-element.127), channel_id=1, source_target_pairs={{0,64},{32,96},{64,0},{96,32},{1,65},{33,97},{65,1},{97,33},{2,66}... | collective-permute-start | bytes 691208 | tf_op jit(solution)/shard_map/ppermute | solution.py:17
  346.1 18.6 %collective-permute-start.114 = (bf16[3,40,960]{2,1,0:T(8,128)(2,1)S(1)}, bf16[3,40,960]{2,1,0:T(8,128)(2,1)S(1)}, u32[]{:S(2)}, u32[]{:S(2)}) collective-permute-start(bf16[3,40,960]{2,1,0:T(8,128)(2,1)S(1)} %get-tuple-element.126), channel_id=1, source_target_pairs={{0,96},{32,0},{64,32},{96,64},{1,97},{33,1},{65,33},{97,65},{2,98}... | collective-permute-start | bytes 691208 | tf_op jit(solution)/shard_map/ppermute | solution.py:17
  346.1 19.1 %collective-permute-start.22 = (bf16[3,40,960]{2,1,0:T(8,128)(2,1)S(1)}, bf16[3,40,960]{2,1,0:T(8,128)(2,1)S(1)}, u32[]{:S(2)}, u32[]{:S(2)}) collective-permute-start(bf16[3,40,960]{2,1,0:T(8,128)(2,1)S(1)} %pad_maximum_fusion.59), channel_id=1, source_target_pairs={{0,96},{32,0},{64,32},{96,64},{1,97},{33,1},{65,33},{97,65},{2,98}... | collective-permute-start | bytes 691208 | tf_op jit(solution)/shard_map/ppermute | solution.py:17
  348.1 17.9 %collective-permute-start.23 = (bf16[3,40,960]{2,1,0:T(8,128)(2,1)S(1)}, bf16[3,40,960]{2,1,0:T(8,128)(2,1)S(1)}, u32[]{:S(2)}, u32[]{:S(2)}) collective-permute-start(bf16[3,40,960]{2,1,0:T(8,128)(2,1)S(1)} %pad_maximum_fusion.59), channel_id=1, source_target_pairs={{0,64},{32,96},{64,0},{96,32},{1,65},{33,97},{65,1},{97,33},{2,66}... | collective-permute-start | bytes 691208 | tf_op jit(solution)/shard_map/ppermute | solution.py:17
  366.0 15.3 %collective-permute-start.84 = (bf16[3,40,960]{2,1,0:T(8,128)(2,1)S(1)}, bf16[3,40,960]{2,1,0:T(8,128)(2,1)S(1)}, u32[]{:S(2)}, u32[]{:S(2)}) collective-permute-start(bf16[3,40,960]{2,1,0:T(8,128)(2,1)S(1)} %pad_maximum_fusion.61), channel_id=1, source_target_pairs={{0,96},{32,0},{64,32},{96,64},{1,97},{33,1},{65,33},{97,65},{2,98}... | collective-permute-start | bytes 691208 | tf_op jit(solution)/shard_map/ppermute | solution.py:17
  383.4 24.7 %collective-permute-start.25 = (bf16[3,160,960]{2,1,0:T(8,128)(2,1)S(1)}, bf16[3,160,960]{2,1,0:T(8,128)(2,1)S(1)}, u32[]{:S(2)}, u32[]{:S(2)}) collective-permute-start(bf16[3,160,960]{2,1,0:T(8,128)(2,1)S(1)} %pad_maximum_fusion.9), channel_id=1, source_target_pairs={{0,16},{16,0},{1,17},{17,1},{2,18},{18,2},{3,19},{19,3},{4,20},{20... | collective-permute-start | bytes 2764808 | tf_op jit(solution)/shard_map/ppermute | solution.py:17
  385.6 41.6 %collective-permute-start.56 = (bf16[3,160,960]{2,1,0:T(8,128)(2,1)S(1)}, bf16[3,160,960]{2,1,0:T(8,128)(2,1)S(1)}, u32[]{:S(2)}, u32[]{:S(2)}) collective-permute-start(bf16[3,160,960]{2,1,0:T(8,128)(2,1)S(1)} %pad_maximum_fusion.11), channel_id=1, source_target_pairs={{0,16},{16,0},{1,17},{17,1},{2,18},{18,2},{3,19},{19,3},{4,20},{20... | collective-permute-start | bytes 2764808 | tf_op jit(solution)/shard_map/ppermute | solution.py:17
  387.0 50.8 %collective-permute-start.87 = (bf16[3,160,960]{2,1,0:T(8,128)(2,1)S(1)}, bf16[3,160,960]{2,1,0:T(8,128)(2,1)S(1)}, u32[]{:S(2)}, u32[]{:S(2)}) collective-permute-start(bf16[3,160,960]{2,1,0:T(8,128)(2,1)S(1)} %pad_maximum_fusion.13), channel_id=1, source_target_pairs={{0,16},{16,0},{1,17},{17,1},{2,18},{18,2},{3,19},{19,3},{4,20},{20... | collective-permute-start | bytes 2764808 | tf_op jit(solution)/shard_map/ppermute | solution.py:17
  391.4 61.7 %collective-permute-start.118 = (bf16[3,160,960]{2,1,0:T(8,128)(2,1)S(1)}, bf16[3,160,960]{2,1,0:T(8,128)(2,1)S(1)}, u32[]{:S(2)}, u32[]{:S(2)}) collective-permute-start(bf16[3,160,960]{2,1,0:T(8,128)(2,1)S(1)} %pad_maximum_fusion.15), channel_id=1, source_target_pairs={{0,16},{16,0},{1,17},{17,1},{2,18},{18,2},{3,19},{19,3},{4,20},{20... | collective-permute-start | bytes 2764808 | tf_op jit(solution)/shard_map/ppermute | solution.py:17
  462.4 20.1 %collective-permute-start.26 = (bf16[256,1024]{1,0:T(8,128)(2,1)}, bf16[256,1024]{1,0:T(8,128)(2,1)}, u32[]{:S(2)}, u32[]{:S(2)}) collective-permute-start(bf16[256,1024]{1,0:T(8,128)(2,1)} %slice.1295), channel_id=1, source_target_pairs={{0,1},{1,0},{2,3},{3,2},{4,5},{5,4},{6,7},{7,6},{8,9},{9,8},{10,11... | collective-permute-start | bytes 1572872 | tf_op jit(solution)/shard_map/ppermute | solution.py:17
  463.2 23.4 %collective-permute-start.57 = (bf16[256,1024]{1,0:T(8,128)(2,1)}, bf16[256,1024]{1,0:T(8,128)(2,1)}, u32[]{:S(2)}, u32[]{:S(2)}) collective-permute-start(bf16[256,1024]{1,0:T(8,128)(2,1)} %slice.1361), channel_id=1, source_target_pairs={{0,1},{1,0},{2,3},{3,2},{4,5},{5,4},{6,7},{7,6},{8,9},{9,8},{10,11... | collective-permute-start | bytes 1572872 | tf_op jit(solution)/shard_map/ppermute | solution.py:17
  465.5 23.3 %collective-permute-start.88 = (bf16[256,1024]{1,0:T(8,128)(2,1)}, bf16[256,1024]{1,0:T(8,128)(2,1)}, u32[]{:S(2)}, u32[]{:S(2)}) collective-permute-start(bf16[256,1024]{1,0:T(8,128)(2,1)} %slice.1427), channel_id=1, source_target_pairs={{0,1},{1,0},{2,3},{3,2},{4,5},{5,4},{6,7},{7,6},{8,9},{9,8},{10,11... | collective-permute-start | bytes 1572872 | tf_op jit(solution)/shard_map/ppermute | solution.py:17
  466.3 26.6 %collective-permute-start.119 = (bf16[256,1024]{1,0:T(8,128)(2,1)}, bf16[256,1024]{1,0:T(8,128)(2,1)}, u32[]{:S(2)}, u32[]{:S(2)}) collective-permute-start(bf16[256,1024]{1,0:T(8,128)(2,1)} %slice.1493), channel_id=1, source_target_pairs={{0,1},{1,0},{2,3},{3,2},{4,5},{5,4},{6,7},{7,6},{8,9},{9,8},{10,11... | collective-permute-start | bytes 1572872 | tf_op jit(solution)/shard_map/ppermute | solution.py:17
  490.0 15.8 %collective-permute-start.89 = (bf16[128,1024]{1,0:T(8,128)(2,1)S(1)}, bf16[128,1024]{1,0:T(8,128)(2,1)S(1)}, u32[]{:S(2)}, u32[]{:S(2)}) collective-permute-start(bf16[128,1024]{1,0:T(8,128)(2,1)S(1)} %slice.1973), channel_id=1, source_target_pairs={{0,8},{8,0},{1,9},{9,1},{2,10},{10,2},{3,11},{11,3},{4,12},{12,4},... | collective-permute-start | bytes 786440 | tf_op jit(solution)/shard_map/ppermute | solution.py:17
  494.1 16.3 %collective-permute-start.120 = (bf16[128,1024]{1,0:T(8,128)(2,1)S(1)}, bf16[128,1024]{1,0:T(8,128)(2,1)S(1)}, u32[]{:S(2)}, u32[]{:S(2)}) collective-permute-start(bf16[128,1024]{1,0:T(8,128)(2,1)S(1)} %slice.1972), channel_id=1, source_target_pairs={{0,8},{8,0},{1,9},{9,1},{2,10},{10,2},{3,11},{11,3},{4,12},{12,4},... | collective-permute-start | bytes 786440 | tf_op jit(solution)/shard_map/ppermute | solution.py:17
  495.1 17.7 %collective-permute-start.28 = (bf16[32,1024]{1,0:T(8,128)(2,1)S(1)}, bf16[32,1024]{1,0:T(8,128)(2,1)S(1)}, u32[]{:S(2)}, u32[]{:S(2)}) collective-permute-start(bf16[32,1024]{1,0:T(8,128)(2,1)S(1)} %get-tuple-element.200), channel_id=1, source_target_pairs={{0,2},{2,4},{4,6},{6,0},{1,3},{3,5},{5,7},{7,1},{8,10},{10,12},{12... | collective-permute-start | bytes 196616 | tf_op jit(solution)/shard_map/ppermute | solution.py:17
  497.0 18.2 %collective-permute-start.29 = (bf16[32,1024]{1,0:T(8,128)(2,1)S(1)}, bf16[32,1024]{1,0:T(8,128)(2,1)S(1)}, u32[]{:S(2)}, u32[]{:S(2)}) collective-permute-start(bf16[32,1024]{1,0:T(8,128)(2,1)S(1)} %get-tuple-element.202), channel_id=1, source_target_pairs={{0,4},{2,6},{4,0},{6,2},{1,5},{3,7},{5,1},{7,3},{8,12},{10,14},{12... | collective-permute-start | bytes 196616 | tf_op jit(solution)/shard_map/ppermute | solution.py:17
  500.1 15.0 %collective-permute-start.30 = (bf16[32,1024]{1,0:T(8,128)(2,1)S(1)}, bf16[32,1024]{1,0:T(8,128)(2,1)S(1)}, u32[]{:S(2)}, u32[]{:S(2)}) collective-permute-start(bf16[32,1024]{1,0:T(8,128)(2,1)S(1)} %get-tuple-element.201), channel_id=1, source_target_pairs={{0,6},{2,0},{4,2},{6,4},{1,7},{3,1},{5,3},{7,5},{8,14},{10,8},{12,... | collective-permute-start | bytes 196616 | tf_op jit(solution)/shard_map/ppermute | solution.py:17
  (134 other events, 2823.1 us)
